TPU v7x, 256 devices: a whole 4x4x8 slice. The times are simulated.
256 devices in a mesh: grp: 4 (over y), seq: 16 (over z, core), head: 4 (over x).
Axes of the slice: x: 4, y: 4, z: 8, core: 2. Of those that a mesh axis runs over, the one named last changes fastest.
Arguments:
- keys: bfloat16 [32, 8192, 1536], P('grp', 'seq', 'head'), may hold values from -6 to 6
- values: bfloat16 [32, 8192, 1536], P('grp', 'seq', 'head'), may hold values from -6 to 6
- log_forget: float32 [32, 24, 8192], P('grp', 'head', 'seq'), may hold values from -0.6 to 0, as said below
- keep: int32 [32, 8192], P('grp', 'seq'), may hold values from 0 to 1, as said below
- merge_weight: float32 [32, 8192], P('grp', 'seq'), may hold values from 0.1 to 10
- lengths: int32 [32], P('grp'), may hold values from 64 to 8192, as said below
- route: int32 [32], P('grp'), may hold values from 0 to 31, as said below
- fresh: bfloat16 [3, 32, 1536], P(None, 'grp', 'head'), may hold values from -7.5 to 7.5
- new_forget: bfloat16 [32, 24], P('grp', 'head'), may hold values from -1 to -0.049804688
- out_weight: bfloat16 [1536, 1536], P('head', 'seq'), may hold values from -0.15625 to 0.15625
Outputs:
- compact_keys: bfloat16 [32, 4096, 1536], P('grp', 'seq', 'head')
- compact_values: bfloat16 [32, 4096, 1536], P('grp', 'seq', 'head')
- compact_decay: float32 [32, 24, 4096], P('grp', 'head', 'seq')
- layer_out: bfloat16 [32, 1536], P('grp', 'seq')
Inputs may be any that keep to these rules, and one draw needn't show every extreme that they name: `keep`: within every aligned block of 64 positions of a request, between 16 and 31 entries are 1, and some block has exactly 31. `lengths`: multiples of 64; the first request of every 8 in order has 8192. `route`: A permutation of the requests. `log_forget`: Negative.
All inputs are finite; a program needn't handle non-finite values.
Results may differ from a plain program's by a relative error of at most 0.0085.
Values may be sent and summed in bfloat16 or wider, within the bound.
A program may use at most 64 MiB of HBM per device.

v0:
```python
import jax
import jax.numpy as jnp
from jax import lax
from jax.sharding import PartitionSpec as P

BLOCK = 64
SLOTS = 32
EMPTY_LOG = -10000.0
HIGHEST = lax.Precision.HIGHEST


def shards(
    keys, values, log_forget, keep, merge_weight, lengths, route, fresh, new_forget, out_weight
):
    f32, bf16 = (jnp.float32, jnp.bfloat16)
    req_dev, pos_dev, width_dev = keys.shape
    heads_dev = log_forget.shape[1]
    head_size = width_dev // heads_dev
    blocks_dev = pos_dev // BLOCK
    rows_dev = blocks_dev * SLOTS
    n_seq = lax.axis_size("seq")
    shard = lax.axis_index("seq")
    grp_req = fresh.shape[1]
    packed_fresh = jnp.concatenate(
        [fresh.transpose(1, 0, 2).reshape(grp_req, 3 * width_dev), new_forget], axis=1
    )
    arrived = lax.all_gather(packed_fresh, "grp", axis=0, tiled=True)
    picked = jnp.take(arrived, route, axis=0)
    query = picked[:, :width_dev]
    own_key = picked[:, width_dev : 2 * width_dev]
    own_value = picked[:, 2 * width_dev : 3 * width_dev].astype(f32)
    new_log = picked[:, 3 * width_dev :].astype(f32)
    position = shard * pos_dev + jnp.arange(pos_dev, dtype=jnp.int32)
    live = position[None, :] < lengths[:, None]
    forget = jnp.where(live[:, None, :], log_forget, 0.0)
    forget_blocks = forget.reshape(req_dev, heads_dev, blocks_dev, BLOCK)
    at = jnp.arange(BLOCK, dtype=jnp.int32)
    after = (at[:, None] > at[None, :]).astype(f32)
    within = jnp.einsum("rhbt,tp->rhbp", forget_blocks, after, precision=HIGHEST)
    block_total = jnp.sum(forget_blocks, axis=3)
    own_total = jnp.sum(block_total, axis=2)
    bt = jnp.arange(blocks_dev, dtype=jnp.int32)
    later_block = jnp.einsum(
        "rhb,bc->rhc", block_total, (bt[:, None] > bt[None, :]).astype(f32), precision=HIGHEST
    )
    totals = lax.all_gather(own_total, "seq")
    later_shard = jnp.sum(
        jnp.where((jnp.arange(n_seq) > shard)[:, None, None], totals, 0.0), axis=0
    )
    decay_blocks = within + later_block[..., None] + later_shard[:, :, None, None]
    flags = keep.reshape(req_dev, blocks_dev, BLOCK)
    upto = (at[:, None] <= at[None, :]).astype(bf16)
    rank = (
        jnp.einsum("rbt,tp->rbp", flags.astype(bf16), upto, preferred_element_type=f32).astype(
            jnp.int32
        )
        - 1
    )
    slot_ids = jnp.arange(SLOTS - 1, dtype=jnp.int32)
    block_start = shard * pos_dev + bt * BLOCK
    block_live = (block_start[None, :] < lengths[:, None]).astype(f32)
    chosen = (
        (flags[:, :, None, :] == 1) & (rank[:, :, None, :] == slot_ids[None, None, :, None])
    ).astype(f32)
    chosen = chosen * block_live[:, :, None, None]
    dropped = flags == 0
    weighted = jnp.where(dropped, merge_weight.reshape(req_dev, blocks_dev, BLOCK), 0.0)
    share = (weighted / jnp.sum(weighted, axis=2, keepdims=True)).astype(bf16).astype(f32)
    merged_row = (share * block_live[:, :, None])[:, :, None, :]
    select = jnp.concatenate([chosen, merged_row], axis=2).astype(bf16)
    key_blocks = keys.reshape(req_dev, blocks_dev, BLOCK, width_dev)
    value_blocks = values.reshape(req_dev, blocks_dev, BLOCK, width_dev)
    packed_keys = (
        jnp.einsum("rbej,rbjc->rbec", select, key_blocks, preferred_element_type=f32)
        .astype(bf16)
        .reshape(req_dev, rows_dev, width_dev)
    )
    packed_values = (
        jnp.einsum("rbej,rbjc->rbec", select, value_blocks, preferred_element_type=f32)
        .astype(bf16)
        .reshape(req_dev, rows_dev, width_dev)
    )
    dealt = lax.all_to_all(
        jnp.stack([packed_keys, packed_values]), "seq", split_axis=2, concat_axis=2, tiled=True
    )
    kept_log = jnp.einsum("rbej,rhbj->rhbe", chosen, decay_blocks, precision=HIGHEST)
    filled = jnp.sum(chosen, axis=3)
    kept_log = kept_log + (1.0 - filled)[:, None, :, :] * EMPTY_LOG
    drop_mask = dropped[:, None, :, :]
    drop_peak = jnp.max(jnp.where(drop_mask, decay_blocks, -jnp.inf), axis=3)
    spread = jnp.where(drop_mask, jnp.exp(decay_blocks - drop_peak[..., None]), 0.0)
    merged_log = drop_peak + jnp.log(jnp.sum(share[:, None, :, :] * spread, axis=3))
    merged_log = jnp.where(block_live[:, None, :] > 0, merged_log, EMPTY_LOG)
    slot_log = jnp.concatenate([kept_log, merged_log[..., None]], axis=3).reshape(
        req_dev, heads_dev, rows_dev
    )
    compact_decay = jnp.exp(slot_log)
    scale = head_size ** (-0.5)
    head_of = jnp.arange(width_dev, dtype=jnp.int32) // head_size
    onehot = head_of[:, None] == jnp.arange(heads_dev, dtype=jnp.int32)[None, :]
    query_blocks = jnp.where(onehot[None], query[:, :, None], jnp.zeros((), bf16))
    scores = (
        jnp.einsum("rnc,rch->rhn", packed_keys, query_blocks, preferred_element_type=f32) * scale
        + slot_log
    )
    local_top = jnp.max(scores, axis=2)
    weights = jnp.exp(scores - local_top[..., None]).astype(bf16)
    local_sum = jnp.sum(weights.astype(f32), axis=2)
    full_acc = jnp.einsum("rhn,rnc->rhc", weights, packed_values, preferred_element_type=f32)
    local_acc = jnp.sum(jnp.where(onehot.T[None], full_acc, 0.0), axis=1)
    stats = jnp.concatenate([local_top, local_sum, local_acc], axis=1)
    every = lax.all_gather(stats, "seq")
    tops = every[:, :, :heads_dev]
    sums = every[:, :, heads_dev : 2 * heads_dev]
    accs = every[:, :, 2 * heads_dev :]
    top = jnp.max(tops, axis=0)
    rescale = jnp.exp(tops - top[None])
    total_sum = jnp.sum(rescale * sums, axis=0)
    total_acc = jnp.sum(jnp.repeat(rescale, head_size, axis=2) * accs, axis=0)
    own_score = (
        jnp.sum(
            (query.astype(f32) * own_key.astype(f32)).reshape(req_dev, heads_dev, head_size), axis=2
        )
        * scale
    )
    cache_top = top + new_log
    joint = jnp.maximum(cache_top, own_score)
    cache_scale = jnp.exp(cache_top - joint)
    self_weight = jnp.exp(own_score - joint)
    numer = (
        jnp.repeat(cache_scale, head_size, axis=1) * total_acc
        + jnp.repeat(self_weight, head_size, axis=1) * own_value
    )
    denom = jnp.repeat(cache_scale * total_sum + self_weight, head_size, axis=1)
    attended = (numer / denom).astype(bf16)
    partial_out = jnp.dot(attended, out_weight, preferred_element_type=f32)
    layer_out = lax.psum(partial_out, "head").astype(bf16)
    return (dealt[0], dealt[1], compact_decay, layer_out)


def solution(mesh):
    return jax.shard_map(
        shards,
        mesh=mesh,
        in_specs=(
            P("grp", "seq", "head"),
            P("grp", "seq", "head"),
            P("grp", "head", "seq"),
            P("grp", "seq"),
            P("grp", "seq"),
            P("grp"),
            P("grp"),
            P(None, "grp", "head"),
            P("grp", "head"),
            P("head", "seq"),
        ),
        out_specs=(
            P("grp", "seq", "head"),
            P("grp", "seq", "head"),
            P("grp", "head", "seq"),
            P("grp", "seq"),
        ),
        check_vma=False,
    )
```

profile of v0, /device:TPU:16, one launch (start us, length us, event | category | flops | bytes accessed | tf_op | source)
XLA Modules:
  0.0 155.7 jit_solution(16878182813551151916)
XLA Ops:
  0.6 0.9 broadcast_compare_fusion.2
  1.5 0.8 convert_element_type.92
  3.1 0.8 reshape.315
  4.3 1.3 broadcast_compare_fusion.3
  7.0 1.7 %copy-done.4 = bf16[8,512,384]{2,1,0:T(8,128)(2,1)S(1)} copy-done((bf16[8,512,384]{2,1,0:T(8,128)(2,1)S(1)}, bf16[8,512,384]{2,1,0:T(8,128)(2,1)}, u32[]{:S(2)}) %copy-start.4) | copy-done | bytes 3145752
  9.3 0.9 copy.48
  10.4 0.9 copy.49
  11.4 2.1 %pad_maximum_fusion = bf16[2,8,256,384]{3,1,0,2:T(8,128)(2,1)} fusion(bf16[1,8,256,384]{3,1,0,2:T(8,128)(2,1)S(1)} %copy.49, bf16[1,8,256,384]{3,1,0,2:T(8,128)(2,1)S(1)} %copy.48), kind=kLoop, calls=%fused_computation.1 | loop fusion | flops 1572864 | bytes 6291456 | tf_op jit(solution)/shard_map/stack | solution.py:84
  13.5 8.8 %all-to-all-start = ((bf16[2,8,256,384]{3,1,0,2:T(8,128)(2,1)}), bf16[2,8,256,384]{3,1,0,2:T(8,128)(2,1)}, u32[]{:S(2)}, u32[]{:S(2)}) async-start(bf16[2,8,256,384]{3,1,0,2:T(8,128)(2,1)} %pad_maximum_fusion), calls=%async_computation | async-start | bytes 6291456 | tf_op jit(solution)/shard_map/all_to_all | solution.py:83
  22.3 10.7 %all_gather.17 = bf16[32,1158]{1,0:T(8,128)(2,1)S(1)} all-gather(bf16[8,1158]{1,0:T(8,128)(2,1)S(1)} %pad_maximum_fusion.5), channel_id=1, replica_groups=mesh['grp'=4,'seq'=16,'head'=4] {'grp'}, dimensions={0}, use_global_device_ids=true | all-gather | bytes 92640 | tf_op jit(solution)/shard_map/all_gather | solution.py:27
  34.6 69.8 %all-gather = f32[128,6]{1,0:T(8,128)S(1)} all-gather(f32[8,6]{1,0:T(8,128)S(1)} %copy.52), channel_id=2, replica_groups=mesh['grp'=4,'seq'=16,'head'=4] {'seq'}, dimensions={0}, use_global_device_ids=true | all-gather | bytes 3264 | tf_op jit(solution)/shard_map/all_gather | solution.py:46
  106.4 0.8 fusion.33
  107.2 1.0 select_reduce_fusion.1
  110.1 2.8 %fusion.5 = f32[8,6,8,31]{3,1,2,0:T(8,128)S(1)} fusion(f32[8,8]{1,0:T(8,128)S(1)} %copy-done.10, s32[8,8,64]{2,1,0:T(8,128)S(1)} %fusion.12, pred[8,8,64]{2,1,0:T(8,128)(4,1)S(1)} %eq.81, f32[8,6,8,64]{3,2,1,0:T(8,128)} %copy-done.5, f32[8,8,31]{2,1,0:T(8,128)S(1)} %subtract_multiply_fusion), kind=kOutput, calls=%fused_computation.11 | convolution fusion | flops 9535104 | bytes 174592 | tf_op jit(solution)/shard_map/rbej,rhbj->rhbe/dot_general | solution.py:86
  113.9 2.0 %fusion.51 = (f32[8,6]{1,0:T(8,128)S(1)}, f32[8,6,256]{2,1,0:T(8,128)S(1)}) fusion(f32[8,6,256]{2,0,1:T(8,128)S(1)} %reshape.319, bf16[8,256,384]{2,1,0:T(8,128)(2,1)} %bitcast.50, pred[384,6]{0,1:T(8,128)(4,1)S(1)} %iota_compare_fusion.4, bf16[8,384]{1,0:T(8,128)(2,1)S(1)} %copy-done.12), kind=kOutput, calls=%fused_computation.102 | convolution fusion | flops 9492432 | bytes 1679808 | tf_op jit(solution)/shard_map/rnc,rch->rhn/dot_general | solution.py:103
  116.6 15.4 %all-gather.1 = f32[128,396]{1,0:T(8,128)S(1)} all-gather(f32[8,396]{1,0:T(8,128)S(1)} %pad_maximum_fusion.6), channel_id=3, replica_groups=mesh['grp'=4,'seq'=16,'head'=4] {'seq'}, dimensions={0}, use_global_device_ids=true | all-gather | bytes 215424 | tf_op jit(solution)/shard_map/all_gather | solution.py:112
  135.0 1.0 broadcast_in_dim.169
  136.0 1.9 %reshape.325 = f32[16,8,384]{2,1,0:T(8,128)} reshape(f32[16,8,6,64]{3,2,1,0:T(8,128)} %broadcast_in_dim.169) | data formatting | bytes 393216 | tf_op jit(solution)/shard_map/reshape | solution.py:119
  137.9 1.0 fusion.20
  138.9 0.9 fusion.35
  139.8 11.1 %psum.7 = bf16[8,96]{1,0:T(8,128)(2,1)} all-reduce(f32[8,96]{1,0:T(8,128)S(1)} %fusion.35), channel_id=1, replica_groups=mesh['grp'=4,'seq'=16,'head'=4] {'head'}, use_global_device_ids=true, to_apply=%region_14.15 | all-reduce | flops 768 | bytes 4608 | tf_op jit(solution)/shard_map/psum | solution.py:137
  150.9 2.2 %slice_bitcast_fusion = (bf16[8,256,384]{2,0,1:T(8,128)(2,1)S(1)}, bf16[8,256,384]{2,0,1:T(8,128)(2,1)S(1)}) fusion(bf16[2,8,256,384]{3,1,0,2:T(8,128)(2,1)} %all-to-all-done), kind=kLoop, calls=%fused_computation.8 | loop fusion | bytes 6291456 | tf_op jit(solution)/shard_map/squeeze | solution.py:138
  153.1 1.3 copy.61
  154.4 1.3 copy.60
  (96 shorter events, 13.5 us)
Async XLA Ops:
  0.6 5.6 %copy-start = (bf16[8,512,384]{2,1,0:T(8,128)(2,1)S(1)}, bf16[8,512,384]{2,1,0:T(8,128)(2,1)}, u32[]{:S(2)}) copy-start(bf16[8,512,384]{2,1,0:T(8,128)(2,1)} %param.11) | copy-start | bytes 9437188
  5.6 1.3 copy-start.9
  5.7 1.2 copy-start.11
  6.2 2.4 %copy-start.4 = (bf16[8,512,384]{2,1,0:T(8,128)(2,1)S(1)}, bf16[8,512,384]{2,1,0:T(8,128)(2,1)}, u32[]{:S(2)}) copy-start(bf16[8,512,384]{2,1,0:T(8,128)(2,1)} %param.10) | copy-start | bytes 9437188
  7.0 3.5 %copy-start.1 = (bf16[8,8,32,384]{3,2,1,0:T(8,128)(2,1)}, bf16[8,8,32,384]{3,2,1,0:T(8,128)(2,1)S(1)}, u32[]{:S(2)}) copy-start(bf16[8,8,32,384]{3,2,1,0:T(8,128)(2,1)S(1)} %convolution_convert_fusion) | copy-start | bytes 4718596
  9.3 1.1 copy-start.3
  13.5 8.8 %copy-start.18 = (s32[8]{0:T(128)S(1)}, s32[8]{0:T(128)}, u32[]{:S(2)}) copy-start(s32[8]{0:T(128)} %param.16) | copy-start | bytes 100
  13.5 8.8 %copy-start.13 = (bf16[3,8,384]{2,1,0:T(8,128)(2,1)S(1)}, bf16[3,8,384]{2,1,0:T(8,128)(2,1)}, u32[]{:S(2)}) copy-start(bf16[3,8,384]{2,1,0:T(8,128)(2,1)} %param.17) | copy-start | bytes 55300
  13.5 8.8 %copy-start.16 = (bf16[8,6]{1,0:T(8,128)(2,1)S(1)}, bf16[8,6]{1,0:T(8,128)(2,1)}, u32[]{:S(2)}) copy-start(bf16[8,6]{1,0:T(8,128)(2,1)} %param.18) | copy-start | bytes 292
  13.5 20.9 %copy-start.17 = (s32[8]{0:T(128)S(1)}, s32[8]{0:T(128)}, u32[]{:S(2)}) copy-start(s32[8]{0:T(128)} %param.15) | copy-start | bytes 100
  13.5 21.0 %copy-start.7 = (f32[8,6,512]{2,0,1:T(8,128)S(1)}, f32[8,6,512]{2,0,1:T(8,128)}, u32[]{:S(2)}) copy-start(f32[8,6,512]{2,0,1:T(8,128)} %param.12) | copy-start | bytes 294916
  13.5 137.3 %all-to-all-start = ((bf16[2,8,256,384]{3,1,0,2:T(8,128)(2,1)}), bf16[2,8,256,384]{3,1,0,2:T(8,128)(2,1)}, u32[]{:S(2)}, u32[]{:S(2)}) async-start(bf16[2,8,256,384]{3,1,0,2:T(8,128)(2,1)} %pad_maximum_fusion), calls=%async_computation | async-start | bytes 6291456 | tf_op jit(solution)/shard_map/all_to_all | solution.py:83
  33.7 0.6 copy-start.6
  106.1 3.2 %copy-start.10 = (f32[8,8]{1,0:T(8,128)S(1)}, f32[8,8]{1,0:T(8,128)}, u32[]{:S(2)}) copy-start(f32[8,8]{1,0:T(8,128)} %copy-done.9) | copy-start | bytes 772
  106.1 3.8 %copy-start.15 = (pred[8,8]{1,0:T(8,128)(4,1)S(1)}, pred[8,8]{1,0:T(8,128)(4,1)}, u32[]{:S(2)}) copy-start(pred[8,8]{1,0:T(8,128)(4,1)} %get-tuple-element.31) | copy-start | bytes 196
  108.2 0.7 copy-start.5
  110.0 4.0 %copy-start.12 = (bf16[8,384]{1,0:T(8,128)(2,1)S(1)}, bf16[8,384]{1,0:T(8,128)(2,1)}, u32[]{:S(2)}) copy-start(bf16[8,384]{1,0:T(8,128)(2,1)} %slice.40) | copy-start | bytes 18436
  113.2 2.9 %copy-start.2 = (bf16[8,8,32,384]{3,2,1,0:T(8,128)(2,1)S(1)}, bf16[8,8,32,384]{3,2,1,0:T(8,128)(2,1)}, u32[]{:S(2)}) copy-start(bf16[8,8,32,384]{3,2,1,0:T(8,128)(2,1)} %copy-done.1) | copy-start | bytes 4718596
  115.9 16.2 %copy-start.14 = (f32[8,6]{1,0:T(8,128)S(1)}, f32[8,6]{1,0:T(8,128)}, u32[]{:S(2)}) copy-start(f32[8,6]{1,0:T(8,128)} %reduce_sum.107) | copy-start | bytes 580
  135.0 3.9 %copy-start.8 = (bf16[384,96]{0,1:T(8,128)(2,1)S(1)}, bf16[384,96]{0,1:T(8,128)(2,1)}, u32[]{:S(2)}) copy-start(bf16[384,96]{0,1:T(8,128)(2,1)} %param.19) | copy-start | bytes 221188
where the time goes:
time: 157 us; the launch traced here: 156 us
  blocking collectives  107 us (68%)
  local copies, waits for them, and re-layouts  18.8 us (12%)
  other arithmetic  11.5 us (7%)
  starting transfers between devices  8.76 us (6%)
  matrix products  8.72 us (6%)
    all_gather x1, blocking collectives, shards(): totals = lax.all_gather(own_total, 'seq')  69.8 us
    all_gather x1, blocking collectives, shards(): every = lax.all_gather(stats, 'seq')  15.4 us
    psum x1, blocking collectives, shards(): layer_out = lax.psum(partial_out, 'head').astype(bf16)  11.1 us
    all_gather x1, blocking collectives, shards(): arrived = lax.all_gather(packed_fresh, 'grp', axis=0, tiled=True)  10.7 us
    all_to_all x1, starting transfers between devices, shards(): lax.all_to_all(jnp.stack([packed_keys, packed_values]), 'seq', split_axis...  8.76 us
    unnamed x40, local copies, waits for them, and re-layouts  5.05 us
  transfers between devices with their start and end apart: 1, of which 0 were waited for; matrix products, arithmetic and copies ran while one was open for 13% of the time, Pallas kernels for 0%

commit v1 on v0

--- a/solution.py
+++ b/solution.py
@@ -24,7 +24,21 @@
     packed_fresh = jnp.concatenate(
         [fresh.transpose(1, 0, 2).reshape(grp_req, 3 * width_dev), new_forget], axis=1
     )
-    arrived = lax.all_gather(packed_fresh, "grp", axis=0, tiled=True)
+    ways, here, step = (lax.axis_size("grp"), lax.axis_index("grp"), packed_fresh.shape[0])
+    shape = [n * ways if d == 0 else n for d, n in enumerate(packed_fresh.shape)]
+    full = lax.dynamic_update_slice_in_dim(
+        jnp.zeros(shape, packed_fresh.dtype), packed_fresh, here * step, axis=0
+    )
+    going_up = going_down = packed_fresh
+    for far in range(1, ways // 2 + 1):
+        going_up = lax.ppermute(going_up, "grp", [(d, (d + 1) % ways) for d in range(ways)])
+        full = lax.dynamic_update_slice_in_dim(full, going_up, (here - far) % ways * step, axis=0)
+        if 2 * far < ways:
+            going_down = lax.ppermute(going_down, "grp", [(d, (d - 1) % ways) for d in range(ways)])
+            full = lax.dynamic_update_slice_in_dim(
+                full, going_down, (here + far) % ways * step, axis=0
+            )
+    arrived = full
     picked = jnp.take(arrived, route, axis=0)
     query = picked[:, :width_dev]
     own_key = picked[:, width_dev : 2 * width_dev]

time: 157 us -> 167 us (1.064); the launches traced: 156 us -> 164 us
  starting transfers between devices: 8.76 us -> 12.1 us
  other arithmetic: 11.5 us -> 13.4 us
    all_gather x1, blocking collectives: 69.8 us -> 81.2 us  [shards(): totals = lax.all_gather(own_total, 'seq')]
    all_gather x1 -> x0, blocking collectives: 10.7 us -> none  [shards(): arrived = lax.all_gather(packed_fresh, 'grp', axis=0, tiled=True)]
    ppermute x0 -> x3, starting transfers between devices: none -> 3.31 us  [the longest x2 2.57 us: shards(): lax.ppermute(going_up, 'grp', [(d, (d + 1) % ways) for d in range(ways)])]
    unnamed x40 -> x28, local copies, waits for them, and re-layouts: 5.05 us -> 4.61 us
  transfers between devices with their start and end apart: 1 -> 4, of which waited for: 0 -> 1; matrix products, arithmetic and copies ran while one was open for 13% -> 20% of each run, Pallas kernels for 0% -> 0%
where the time goes in v1:
time: 167 us; the launch traced here: 164 us
  blocking collectives  108 us (65%)
  local copies, waits for them, and re-layouts  20 us (12%)
  other arithmetic  13.4 us (8%)
  starting transfers between devices  12.1 us (7%)
  matrix products  8.31 us (5%)
    all_gather x1, blocking collectives, shards(): totals = lax.all_gather(own_total, 'seq')  81.2 us
    all_gather x1, blocking collectives, shards(): every = lax.all_gather(stats, 'seq')  15.4 us
    psum x1, blocking collectives, shards(): layer_out = lax.psum(partial_out, 'head').astype(bf16)  11 us
    all_to_all x1, starting transfers between devices, shards(): lax.all_to_all(jnp.stack([packed_keys, packed_values]), 'seq', split_axis...  8.75 us
    unnamed x28, local copies, waits for them, and re-layouts  4.61 us
  transfers between devices with their start and end apart: 4, of which 1 were waited for; matrix products, arithmetic and copies ran while one was open for 20% of the time, Pallas kernels for 0%

profile of v1, /device:TPU:16, one launch (start us, length us, event | category | flops | bytes accessed | tf_op | source)
XLA Modules:
  0.0 163.7 jit_solution(9602401355627101972)
XLA Ops:
  0.7 1.5 pad_maximum_fusion.5
  2.2 1.3 collective-permute-start
  7.7 1.3 broadcast_compare_fusion.3
  10.3 1.7 %copy-done.4 = bf16[8,512,384]{2,1,0:T(8,128)(2,1)S(1)} copy-done((bf16[8,512,384]{2,1,0:T(8,128)(2,1)S(1)}, bf16[8,512,384]{2,1,0:T(8,128)(2,1)}, u32[]{:S(2)}) %copy-start.4) | copy-done | bytes 3145752
  14.7 2.1 %pad_maximum_fusion = bf16[2,8,256,384]{3,1,0,2:T(8,128)(2,1)} fusion(bf16[1,8,256,384]{3,1,0,2:T(8,128)(2,1)S(1)} %copy.49, bf16[1,8,256,384]{3,1,0,2:T(8,128)(2,1)S(1)} %copy.48), kind=kLoop, calls=%fused_computation.1 | loop fusion | flops 1572864 | bytes 6291456 | tf_op jit(solution)/shard_map/stack | solution.py:98
  16.8 8.7 %all-to-all-start = ((bf16[2,8,256,384]{3,1,0,2:T(8,128)(2,1)}), bf16[2,8,256,384]{3,1,0,2:T(8,128)(2,1)}, u32[]{:S(2)}, u32[]{:S(2)}) async-start(bf16[2,8,256,384]{3,1,0,2:T(8,128)(2,1)} %pad_maximum_fusion), calls=%async_computation | async-start | bytes 6291456 | tf_op jit(solution)/shard_map/all_to_all | solution.py:97
  26.5 81.2 %all-gather = f32[128,6]{1,0:T(8,128)S(1)} all-gather(f32[8,6]{1,0:T(8,128)S(1)} %copy.52), channel_id=2, replica_groups=mesh['grp'=4,'seq'=16,'head'=4] {'seq'}, dimensions={0}, use_global_device_ids=true | all-gather | bytes 3264 | tf_op jit(solution)/shard_map/all_gather | solution.py:60
  108.1 1.0 reshape.318
  109.7 1.0 multiply_reduce_fusion
  111.1 1.2 select_reduce_fusion
  113.1 2.8 %fusion.5 = f32[8,6,8,31]{3,1,2,0:T(8,128)S(1)} fusion(f32[8,8]{1,0:T(8,128)} %copy-done.9, s32[8,8,64]{2,1,0:T(8,128)S(1)} %fusion.12, pred[8,8,64]{2,1,0:T(8,128)(4,1)} %copy-done.8, f32[8,6,8,64]{3,2,1,0:T(8,128)} %copy-done.5, f32[8,8,31]{2,1,0:T(8,128)S(1)} %subtract_multiply_fusion), kind=kOutput, calls=%fused_computation.11 | convolution fusion | flops 9535104 | bytes 174592 | tf_op jit(solution)/shard_map/rbej,rhbj->rhbe/dot_general | solution.py:100
  117.0 1.0 reshape.319
  118.6 1.3 collective-permute-start.2
  121.4 1.2 collective-permute-done.2
  123.5 2.1 %fusion.51 = (f32[8,6]{1,0:T(8,128)S(1)}, f32[8,6,256]{2,1,0:T(8,128)S(1)}) fusion(f32[8,6,256]{2,0,1:T(8,128)S(1)} %reshape.319, bf16[8,256,384]{2,1,0:T(8,128)(2,1)} %bitcast.50, pred[384,6]{0,1:T(8,128)(4,1)S(1)} %iota_compare_fusion.4, bf16[8,384]{1,0:T(8,128)(2,1)S(1)} %slice.40), kind=kOutput, calls=%fused_computation.106 | convolution fusion | flops 9492432 | bytes 1679808 | tf_op jit(solution)/shard_map/rnc,rch->rhn/dot_general | solution.py:117
  126.2 15.4 %all-gather.1 = f32[128,396]{1,0:T(8,128)S(1)} all-gather(f32[8,396]{1,0:T(8,128)S(1)} %pad_maximum_fusion.6), channel_id=3, replica_groups=mesh['grp'=4,'seq'=16,'head'=4] {'seq'}, dimensions={0}, use_global_device_ids=true | all-gather | bytes 215424 | tf_op jit(solution)/shard_map/all_gather | solution.py:126
  142.8 1.0 broadcast_in_dim.173
  143.8 1.9 %reshape.325 = f32[16,8,384]{2,1,0:T(8,128)} reshape(f32[16,8,6,64]{3,2,1,0:T(8,128)} %broadcast_in_dim.173) | data formatting | bytes 393216 | tf_op jit(solution)/shard_map/reshape | solution.py:133
  145.6 1.0 fusion.20
  146.7 1.0 fusion.35
  147.7 11.0 %psum.7 = bf16[8,96]{1,0:T(8,128)(2,1)} all-reduce(f32[8,96]{1,0:T(8,128)S(1)} %fusion.35), channel_id=1, replica_groups=mesh['grp'=4,'seq'=16,'head'=4] {'head'}, use_global_device_ids=true, to_apply=%region_14.15 | all-reduce | flops 768 | bytes 4608 | tf_op jit(solution)/shard_map/psum | solution.py:151
  158.8 2.2 %slice_bitcast_fusion = (bf16[8,256,384]{2,0,1:T(8,128)(2,1)S(1)}, bf16[8,256,384]{2,0,1:T(8,128)(2,1)S(1)}) fusion(bf16[2,8,256,384]{3,1,0,2:T(8,128)(2,1)} %all-to-all-done), kind=kLoop, calls=%fused_computation.8 | loop fusion | bytes 6291456 | tf_op jit(solution)/shard_map/squeeze | solution.py:152
  161.0 1.3 copy.61
  162.3 1.3 copy.60
  (93 shorter events, 17.0 us)
Async XLA Ops:
  0.6 8.9 %copy-start = (bf16[8,512,384]{2,1,0:T(8,128)(2,1)S(1)}, bf16[8,512,384]{2,1,0:T(8,128)(2,1)}, u32[]{:S(2)}) copy-start(bf16[8,512,384]{2,1,0:T(8,128)(2,1)} %param.11) | copy-start | bytes 9437188
  2.2 116.5 %collective-permute-start = (bf16[8,1158]{1,0:T(8,128)(2,1)}, bf16[8,1158]{1,0:T(8,128)(2,1)}, u32[]{:S(2)}, u32[]{:S(2)}) collective-permute-start(bf16[8,1158]{1,0:T(8,128)(2,1)} %get-tuple-element.31), channel_id=1, source_target_pairs={{0,64},{64,128},{128,192},{192,0},{1,65},{65,129},{129,193},{193,1... | collective-permute-start | bytes 55592 | tf_op jit(solution)/shard_map/ppermute | solution.py:34
  3.5 117.2 %collective-permute-start.1 = (bf16[8,1158]{1,0:T(8,128)(2,1)}, bf16[8,1158]{1,0:T(8,128)(2,1)}, u32[]{:S(2)}, u32[]{:S(2)}) collective-permute-start(bf16[8,1158]{1,0:T(8,128)(2,1)} %get-tuple-element.31), channel_id=1, source_target_pairs={{0,192},{64,0},{128,64},{192,128},{1,193},{65,1},{129,65},{193,129... | collective-permute-start | bytes 55592 | tf_op jit(solution)/shard_map/ppermute | solution.py:37
  7.3 3.0 %copy-start.8 = (pred[8,8,64]{2,1,0:T(8,128)(4,1)}, pred[8,8,64]{2,1,0:T(8,128)(4,1)S(1)}, u32[]{:S(2)}) copy-start(pred[8,8,64]{2,1,0:T(8,128)(4,1)S(1)} %eq.85) | copy-start | bytes 12292
  7.6 101.8 %copy-start.6 = (pred[8,8,64]{2,1,0:T(8,128)(4,1)}, pred[8,8,64]{2,1,0:T(8,128)(4,1)S(1)}, u32[]{:S(2)}) copy-start(pred[8,8,64]{2,1,0:T(8,128)(4,1)S(1)} %eq.91) | copy-start | bytes 12292
  9.0 1.3 copy-start.9
  9.6 2.4 %copy-start.4 = (bf16[8,512,384]{2,1,0:T(8,128)(2,1)S(1)}, bf16[8,512,384]{2,1,0:T(8,128)(2,1)}, u32[]{:S(2)}) copy-start(bf16[8,512,384]{2,1,0:T(8,128)(2,1)} %param.10) | copy-start | bytes 9437188
  10.3 3.5 %copy-start.1 = (bf16[8,8,32,384]{3,2,1,0:T(8,128)(2,1)}, bf16[8,8,32,384]{3,2,1,0:T(8,128)(2,1)S(1)}, u32[]{:S(2)}) copy-start(bf16[8,8,32,384]{3,2,1,0:T(8,128)(2,1)S(1)} %convolution_convert_fusion) | copy-start | bytes 4718596
  12.6 1.1 copy-start.3
  16.8 8.9 %copy-start.11 = (s32[8]{0:T(128)S(1)}, s32[8]{0:T(128)}, u32[]{:S(2)}) copy-start(s32[8]{0:T(128)} %param.15) | copy-start | bytes 100
  16.8 9.0 %copy-start.7 = (f32[8,6,512]{2,0,1:T(8,128)S(1)}, f32[8,6,512]{2,0,1:T(8,128)}, u32[]{:S(2)}) copy-start(f32[8,6,512]{2,0,1:T(8,128)} %param.12) | copy-start | bytes 294916
  16.8 141.9 %all-to-all-start = ((bf16[2,8,256,384]{3,1,0,2:T(8,128)(2,1)}), bf16[2,8,256,384]{3,1,0,2:T(8,128)(2,1)}, u32[]{:S(2)}, u32[]{:S(2)}) async-start(bf16[2,8,256,384]{3,1,0,2:T(8,128)(2,1)} %pad_maximum_fusion), calls=%async_computation | async-start | bytes 6291456 | tf_op jit(solution)/shard_map/all_to_all | solution.py:97
  109.7 1.0 copy-start.5
  111.1 5.0 %copy-start.12 = (s32[8]{0:T(128)S(1)}, s32[8]{0:T(128)}, u32[]{:S(2)}) copy-start(s32[8]{0:T(128)} %param.16) | copy-start | bytes 100
  118.6 4.0 %collective-permute-start.2 = (bf16[8,1158]{1,0:T(8,128)(2,1)}, bf16[8,1158]{1,0:T(8,128)(2,1)S(1)}, u32[]{:S(2)}, u32[]{:S(2)}) collective-permute-start(bf16[8,1158]{1,0:T(8,128)(2,1)} %collective-permute-done), channel_id=1, source_target_pairs={{0,64},{64,128},{128,192},{192,0},{1,65},{65,129},{129,193},{193,1... | collective-permute-start | bytes 55592 | tf_op jit(solution)/shard_map/ppermute | solution.py:34
  123.5 2.3 %copy-start.2 = (bf16[8,8,32,384]{3,2,1,0:T(8,128)(2,1)S(1)}, bf16[8,8,32,384]{3,2,1,0:T(8,128)(2,1)}, u32[]{:S(2)}) copy-start(bf16[8,8,32,384]{3,2,1,0:T(8,128)(2,1)} %copy-done.1) | copy-start | bytes 4718596
  142.8 3.9 %copy-start.10 = (f32[8,384]{1,0:T(8,128)S(1)}, f32[8,384]{1,0:T(8,128)}, u32[]{:S(2)}) copy-start(f32[8,384]{1,0:T(8,128)} %reshape.326) | copy-start | bytes 36868
